TPU v7x, 32 devices: a whole 2x2x4 slice. The times are simulated.
32 devices in a mesh: groups: 2 (over y), blk: 4 (over z), sub: 4 (over x, core).
Axes of the slice: x: 2, y: 2, z: 4, core: 2. Of those that a mesh axis runs over, the one named last changes fastest.
Arguments:
- strain: bfloat16 [4096, 2048], P(('groups', 'blk', 'sub')), parts along dimension 0, may hold values from -500 to 500, as said below
- fir_taps: bfloat16 [128], replicated, may hold values from -0.5 to 0.5
- live_mask: int32 [4096], P(('groups', 'blk')), parts along dimension 0, may hold values 0 or 1
- offset_band: int32 [8, 3, 2], P(('groups', 'blk')), parts along dimension 0, may hold values from -1023 to 1023, as said below
Outputs:
- noise_stack: float32 [8, 16, 2048], P(('groups', 'blk'), 'sub'), parts along dimension 0
There are 2 independent parts, one for each index of `groups`. A program takes and returns all parts, laid end to end along the dimension named above; an argument that names none is the same for every part. Nothing has to cross between parts.
Inputs may be any that keep to these rules, and one draw needn't show every extreme that they name: `strain`: strain of every channel, of varying strength from channel to channel and over time. For pair index r (distance d = r - 1) offset_band[i, r, 0] <= offset_band[i, r, 1], both within d * 512 - 511 and d * 512 + 511.
All inputs are finite; a program needn't handle non-finite values. No bound on the sum of `live_mask` on one device may be relied on, other than what follows from the above.
Results may differ from a plain program's by a relative error of at most 0.0029.
Values may be sent and summed in bfloat16 or wider, within the bound.
A program may use at most 64 MiB of HBM per device.

v0:
```python
import functools
import math

import jax
import jax.numpy as jnp
from jax import lax
from jax.experimental import pallas as pl
from jax.experimental.pallas import tpu as pltpu
from jax.sharding import PartitionSpec as P

PANEL = 512
DEC = 4
TAPS = 128
LAGS = 16
LANES = 128
MESH = pl.DeviceIdType.MESH


def shift_right(chunks, amount):
    lane = lax.broadcasted_iota(jnp.int32, chunks[0].shape, 1)
    rolled = [pltpu.roll(chunk, amount, 1) for chunk in chunks]
    before = [jnp.zeros_like(chunks[0])] + rolled[:-1]
    return [jnp.where(lane < amount, b, r) for b, r in zip(before, rolled)]


def diagonal_totals(matrix):
    blocks = PANEL // LANES
    chunks = []
    for j in range(1 - blocks, blocks):
        total = None
        for row in range(max(0, -j), min(blocks, blocks - j)):
            piece = matrix[
                row * LANES : (row + 1) * LANES, (row + j) * LANES : (row + j + 1) * LANES
            ]
            total = piece if total is None else total + piece
        chunks.append(total)
    chunks.append(jnp.zeros_like(chunks[0]))
    half = LANES // 2
    while half >= 8:
        low = shift_right([chunk[:half] for chunk in chunks], half)
        chunks = [a + b[half : 2 * half] for a, b in zip(low, chunks)]
        half //= 2
    row = lax.broadcasted_iota(jnp.int32, chunks[0].shape, 0)
    for bit in (4, 2, 1):
        moved = shift_right(chunks, bit)
        chunks = [jnp.where((row & bit) == 0, m, c) for m, c in zip(moved, chunks)]
    return jnp.concatenate([jnp.sum(c, axis=0, keepdims=True) for c in chunks], axis=1)


def filtered_normalized(strain_ref, taps_ref, own_live):
    channels, raw_length = strain_ref.shape
    time_length = raw_length // DEC
    span = LANES * DEC
    taps = jnp.concatenate([taps_ref[...], jnp.zeros((1, span), jnp.float32)], axis=1)
    bank = jnp.broadcast_to(taps, (LANES, span + TAPS))
    bank = pltpu.roll(bank, DEC, 1, stride=DEC, stride_axis=0).astype(jnp.bfloat16)
    pieces = []
    for block in range(time_length // LANES):
        if block == 0:
            window = jnp.concatenate(
                [jnp.zeros((channels, TAPS), jnp.bfloat16), strain_ref[:, :span]], axis=1
            )
        else:
            window = strain_ref[:, block * span - TAPS : (block + 1) * span]
        pieces.append(
            lax.dot_general(
                window, bank, (((1,), (1,)), ((), ())), preferred_element_type=jnp.float32
            )
        )
    filtered = jnp.concatenate(pieces, axis=1)
    mean_square = jnp.mean(filtered * filtered, axis=1, keepdims=True)
    return (own_live * (filtered / jnp.sqrt(mean_square + 1e-6))).astype(jnp.bfloat16)


def kernel(
    panel_count,
    sub_count,
    reach,
    strain_ref,
    taps_ref,
    live_ref,
    band_ref,
    out_ref,
    panels,
    lives,
    lagged,
    across_send,
    partner_send,
    along_send,
    live_send,
    arrival,
    live_arrival,
):
    channels = strain_ref.shape[0]
    time_length = strain_ref.shape[1] // DEC
    chip_count = sub_count // 2
    lag_count = LAGS // sub_count
    position = lax.axis_index("blk")
    me = lax.axis_index("sub")
    core = lax.rem(me, 2)
    chip = lax.div(me, 2)
    partner = chip * 2 + 1 - core
    distances = [d for step in range(1, reach + 1) for d in (-step, step)]

    def inside(d):
        return jnp.logical_and(position + d >= 0, position + d < panel_count)

    def chip_at(step):
        return lax.rem(chip + step, chip_count)

    barrier = pltpu.get_barrier_semaphore()
    pl.semaphore_signal(barrier, inc=1, device_id={"sub": partner}, device_id_type=MESH)
    for step in range(1, chip_count):
        pl.semaphore_signal(
            barrier, inc=1, device_id={"sub": chip_at(step) * 2 + core}, device_id_type=MESH
        )
    for d in distances:

        @pl.when(inside(d))
        def _():
            pl.semaphore_signal(
                barrier, inc=1, device_id={"blk": position + d}, device_id_type=MESH
            )

    row = lax.broadcasted_iota(jnp.int32, (channels, PANEL), 0)
    column = lax.broadcasted_iota(jnp.int32, (channels, PANEL), 1)
    live_row = live_ref[...].astype(jnp.float32)
    own_live = jnp.sum(
        jnp.where(column == row + me * channels, live_row, 0.0), axis=1, keepdims=True
    )
    panels[reach, me] = filtered_normalized(strain_ref, taps_ref, own_live)

    pl.semaphore_wait(
        barrier,
        chip_count
        + jnp.minimum(position, reach)
        + jnp.minimum(panel_count - 1 - position, reach),
    )

    def across(step):
        return pltpu.make_async_remote_copy(
            src_ref=panels.at[reach, me],
            dst_ref=panels.at[reach, me],
            send_sem=across_send.at[step],
            recv_sem=arrival.at[reach, me],
            device_id={"sub": chip_at(step) * 2 + core},
            device_id_type=MESH,
        )

    def to_partner(d, step):
        shard = chip_at(step) * 2 + core
        return pltpu.make_async_remote_copy(
            src_ref=panels.at[d + reach, shard],
            dst_ref=panels.at[d + reach, shard],
            send_sem=partner_send.at[d + reach, step],
            recv_sem=arrival.at[d + reach, shard],
            device_id={"sub": partner},
            device_id_type=MESH,
        )

    def along(d, step):
        shard = chip_at(step) * 2 + core
        return pltpu.make_async_remote_copy(
            src_ref=panels.at[reach, shard],
            dst_ref=panels.at[reach - d, shard],
            send_sem=along_send.at[d + reach, step],
            recv_sem=arrival.at[reach - d, shard],
            device_id={"blk": position + d},
            device_id_type=MESH,
        )

    def along_live(d):
        return pltpu.make_async_remote_copy(
            src_ref=live_ref,
            dst_ref=lives.at[reach - d],
            send_sem=live_send.at[d + reach],
            recv_sem=live_arrival.at[reach - d],
            device_id={"blk": position + d},
            device_id_type=MESH,
        )

    def arrived(d, shard):
        pltpu.make_async_copy(
            panels.at[d + reach, shard], panels.at[d + reach, shard], arrival.at[d + reach, shard]
        ).wait()

    for step in range(1, chip_count):
        across(step).start()
    for d in distances:

        @pl.when(inside(d))
        def _():
            along(d, 0).start()
            along_live(d).start()

    to_partner(0, 0).start()

    own_row = lax.broadcasted_iota(jnp.int32, (PANEL, PANEL), 0)
    own_column = lax.broadcasted_iota(jnp.int32, (PANEL, PANEL), 1)
    live_column = jnp.sum(
        jnp.where(own_row == own_column, live_row, 0.0), axis=1, keepdims=True
    )
    out_ref[...] = jnp.zeros_like(out_ref)

    for step in range(1, chip_count):
        arrived(0, chip_at(step) * 2 + core)
        to_partner(0, step).start()
        for d in distances:

            @pl.when(inside(d))
            def _():
                along(d, step).start()

    for d in distances:

        @pl.when(inside(d))
        def _():
            arrived(d, me)
            to_partner(d, 0).start()

    for step in range(chip_count):
        arrived(0, chip_at(step) * 2 + 1 - core)

    first_lag = me * lag_count
    own = panels[reach].reshape(PANEL, time_length).astype(jnp.float32)
    chunks = [own[:, i : i + LANES] for i in range(0, time_length, LANES)]
    chunks = shift_right(chunks, first_lag)
    for lag in range(lag_count):
        if lag:
            chunks = shift_right(chunks, 1)
        lagged[lag] = jnp.concatenate(chunks, axis=1).astype(jnp.bfloat16)

    def correlate(d):
        visiting = panels[d + reach].reshape(PANEL, time_length)
        rows = []
        for lag in range(lag_count):
            correlation = lax.dot_general(
                lagged[lag],
                visiting,
                (((1,), (1,)), ((), ())),
                preferred_element_type=jnp.float32,
            )
            rows.append(diagonal_totals(correlation))
        flags = live_ref[...] if d == 0 else lives[d + reach]
        rows.append(diagonal_totals(live_column * flags.astype(jnp.float32)))
        totals = jnp.concatenate(rows, axis=0)
        offset = (
            lax.broadcasted_iota(jnp.int32, totals.shape, 1) + d * PANEL - (PANEL - 1)
        )
        kept = jnp.logical_and(
            offset >= band_ref[0, d + reach, 0], offset <= band_ref[0, d + reach, 1]
        )
        kept = jnp.logical_and(kept, offset < d * PANEL + PANEL)
        start = (d + reach) * PANEL
        window = (slice(0, lag_count + 1), slice(start, start + 2 * PANEL))
        out_ref[window] += jnp.where(kept, totals, 0.0)

    correlate(0)

    for step in range(1, chip_count):
        for d in distances:

            @pl.when(inside(d))
            def _():
                arrived(d, chip_at(step) * 2 + core)
                to_partner(d, step).start()

    for d in distances:

        @pl.when(inside(d))
        def _():
            for step in range(chip_count):
                arrived(d, chip_at(step) * 2 + 1 - core)
            pltpu.make_async_copy(
                lives.at[d + reach], lives.at[d + reach], live_arrival.at[d + reach]
            ).wait()
            correlate(d)

    for step in range(1, chip_count):
        across(step).wait_send()
    for step in range(chip_count):
        to_partner(0, step).wait_send()
    for d in distances:

        @pl.when(inside(d))
        def _():
            along_live(d).wait_send()
            for step in range(chip_count):
                along(d, step).wait_send()
                to_partner(d, step).wait_send()


def on_device(strain, fir_taps, live_mask, offset_band):
    channels, raw_length = strain.shape
    time_length = raw_length // DEC
    panel_count = lax.axis_size("blk")
    sub_count = lax.axis_size("sub")
    reach = max(1, panel_count // 8)
    slots = 2 * reach + 1
    chip_count = sub_count // 2
    lag_count = LAGS // sub_count
    width = (2 * reach + 2) * PANEL
    vmem = pl.BlockSpec(memory_space=pltpu.VMEM)
    dma = pltpu.SemaphoreType.DMA
    sums = pl.pallas_call(
        functools.partial(kernel, panel_count, sub_count, reach),
        out_shape=jax.ShapeDtypeStruct((8, width), jnp.float32),
        in_specs=[vmem, vmem, vmem, pl.BlockSpec(memory_space=pltpu.SMEM)],
        out_specs=vmem,
        scratch_shapes=[
            pltpu.VMEM((slots, sub_count, channels, time_length), jnp.bfloat16),
            pltpu.VMEM((slots, 1, PANEL), jnp.int32),
            pltpu.VMEM((lag_count, PANEL, time_length), jnp.bfloat16),
            dma((chip_count,)),
            dma((slots, chip_count)),
            dma((slots, chip_count)),
            dma((slots,)),
            dma((slots, sub_count)),
            dma((slots,)),
        ],
        compiler_params=pltpu.CompilerParams(collective_id=0, has_side_effects=True),
    )(
        strain,
        fir_taps.astype(jnp.float32).reshape(1, TAPS),
        live_mask.reshape(1, PANEL),
        offset_band,
    )
    stack, count = sums[:lag_count], sums[lag_count : lag_count + 1]
    return (stack / jnp.maximum(count, 1.0) / math.sqrt(time_length))[None]


def solution(mesh):
    in_specs = (
        P(("groups", "blk", "sub"), None),
        P(),
        P(("groups", "blk")),
        P(("groups", "blk"), None, None),
    )
    out_specs = P(("groups", "blk"), "sub", None)
    return jax.shard_map(
        on_device, mesh=mesh, in_specs=in_specs, out_specs=out_specs, check_vma=False
    )
```

profile of v0, /device:TPU:9, one launch (start us, length us, event | category | flops | bytes accessed | tf_op | source)
XLA Modules:
  0.0 21.1 jit_solution(1373403701154263735)
XLA Ops:
  0.0 0.0 copy-start.1
  0.0 0.7 %copy-done.1 = bf16[128]{0:T(256)(128)(2,1)S(1)} copy-done((bf16[128]{0:T(256)(128)(2,1)S(1)}, bf16[128]{0:T(256)(128)(2,1)}, u32[]{:S(2)}) %copy-start.1) | copy-done | bytes 280
  0.7 0.0 copy-start
  0.7 0.5 %bitcast_convert_fusion.taps_ref = f32[1,128]{1,0:T(1,128)} fusion(bf16[128]{0:T(256)(128)(2,1)S(1)} %copy-done.1), kind=kLoop, calls=%fused_computation.2 | loop fusion | flops 128 | bytes 768 | tf_op jit(solution)/shard_map/reshape | solution.py:324
  1.2 0.2 copy-done
  1.3 0.7 %copy.5.band_ref = s32[1,3,2]{2,1,0:T(4,128)} copy(s32[1,3,2]{1,2,0:T(2,128)S(1)} %copy-done) | data formatting | bytes 48 | tf_op args[3]
  2.0 16.8 %shard_map.46 = f32[8,2048]{1,0:T(8,128)} custom-call(bf16[128,2048]{1,0:T(8,128)(2,1)} %strain_ref.1, f32[1,128]{1,0:T(1,128)} %bitcast_convert_fusion.taps_ref, s32[1,512]{1,0:T(1,128)} %bitcast.8, s32[1,3,2]{2,1,0:T(4,128)} %copy.5.band_ref), custom_call_target="tpu_custom_call" | custom-call | tf_op jit(solution)/shard_map/pallas_call | solution.py:305
  18.8 0.9 %slice_maximum_fusion = f32[1,2048]{1,0:T(1,128)S(1)} fusion(f32[8,2048]{1,0:T(8,128)} %shard_map.46), kind=kLoop, calls=%fused_computation.1 | loop fusion | flops 2048 | bytes 16384 | tf_op jit(solution)/shard_map/max | solution.py:329
  19.7 1.5 %multiply_bitcast_fusion = f32[1,4,2048]{2,1,0:T(4,128)} fusion(f32[8,2048]{1,0:T(8,128)} %shard_map.46, f32[2048]{0:T(1024)S(1)} %bitcast.7), kind=kLoop, calls=%fused_computation | loop fusion | flops 16384 | bytes 73728 | tf_op jit(solution)/shard_map/broadcast_in_dim | solution.py:329
Async XLA Ops:
  0.0 0.7 %copy-start.1 = (bf16[128]{0:T(256)(128)(2,1)S(1)}, bf16[128]{0:T(256)(128)(2,1)}, u32[]{:S(2)}) copy-start(bf16[128]{0:T(256)(128)(2,1)} %param.5) | copy-start | bytes 772
  0.7 0.7 %copy-start = (s32[1,3,2]{1,2,0:T(2,128)S(1)}, s32[1,3,2]{1,2,0:T(2,128)}, u32[]{:S(2)}) copy-start(s32[1,3,2]{1,2,0:T(2,128)} %param.7) | copy-start | bytes 76
where the time goes:
time: 21.5 us; the launch traced here: 21.1 us
  Pallas kernels  16.8 us (78%)
  other arithmetic  2.83 us (13%)
  local copies, waits for them, and re-layouts  1.49 us (7%)
    pallas_call x1, Pallas kernels, on_device(): pl.pallas_call(functools.partial(kernel, panel_count, sub_count, reach),...  16.8 us
    unnamed x5, local copies, waits for them, and re-layouts  1.49 us
    broadcast_in_dim x1, other arithmetic, on_device(): return (stack / jnp.maximum(count, 1.0) / math.sqrt(time_length))[None]  1.47 us
    max x1, other arithmetic, on_device(): return (stack / jnp.maximum(count, 1.0) / math.sqrt(time_length))[None]  0.85 us
    reshape x1, other arithmetic, on_device(): fir_taps.astype(jnp.float32).reshape(1, TAPS)  0.51 us

commit v1 on v0

--- a/solution.py
+++ b/solution.py
@@ -51,7 +51,7 @@
     channels, raw_length = strain_ref.shape
     time_length = raw_length // DEC
     span = LANES * DEC
-    taps = jnp.concatenate([taps_ref[...], jnp.zeros((1, span), jnp.float32)], axis=1)
+    taps = jnp.concatenate([taps_ref[...].astype(jnp.float32).reshape(1, TAPS), jnp.zeros((1, span), jnp.float32)], axis=1)
     bank = jnp.broadcast_to(taps, (LANES, span + TAPS))
     bank = pltpu.roll(bank, DEC, 1, stride=DEC, stride_axis=0).astype(jnp.bfloat16)
     pieces = []
@@ -84,6 +84,7 @@
     panels,
     lives,
     lagged,
+    sums,
     across_send,
     partner_send,
     along_send,
@@ -200,7 +201,7 @@
     live_column = jnp.sum(
         jnp.where(own_row == own_column, live_row, 0.0), axis=1, keepdims=True
     )
-    out_ref[...] = jnp.zeros_like(out_ref)
+    sums[...] = jnp.zeros_like(sums)
 
     for step in range(1, chip_count):
         arrived(0, chip_at(step) * 2 + core)
@@ -248,12 +249,12 @@
             lax.broadcasted_iota(jnp.int32, totals.shape, 1) + d * PANEL - (PANEL - 1)
         )
         kept = jnp.logical_and(
-            offset >= band_ref[0, d + reach, 0], offset <= band_ref[0, d + reach, 1]
+            offset >= band_ref[0, 0, d + reach], offset <= band_ref[0, 1, d + reach]
         )
         kept = jnp.logical_and(kept, offset < d * PANEL + PANEL)
         start = (d + reach) * PANEL
         window = (slice(0, lag_count + 1), slice(start, start + 2 * PANEL))
-        out_ref[window] += jnp.where(kept, totals, 0.0)
+        sums[window] += jnp.where(kept, totals, 0.0)
 
     correlate(0)
 
@@ -275,6 +276,9 @@
                 lives.at[d + reach], lives.at[d + reach], live_arrival.at[d + reach]
             ).wait()
             correlate(d)
+
+    inverse = 1.0 / (jnp.maximum(sums[lag_count:], 1.0) * math.sqrt(time_length))
+    out_ref[0] = sums[:lag_count] * inverse
 
     for step in range(1, chip_count):
         across(step).wait_send()
@@ -302,15 +306,16 @@
     width = (2 * reach + 2) * PANEL
     vmem = pl.BlockSpec(memory_space=pltpu.VMEM)
     dma = pltpu.SemaphoreType.DMA
-    sums = pl.pallas_call(
+    return pl.pallas_call(
         functools.partial(kernel, panel_count, sub_count, reach),
-        out_shape=jax.ShapeDtypeStruct((8, width), jnp.float32),
+        out_shape=jax.ShapeDtypeStruct((1, lag_count, width), jnp.float32),
         in_specs=[vmem, vmem, vmem, pl.BlockSpec(memory_space=pltpu.SMEM)],
         out_specs=vmem,
         scratch_shapes=[
             pltpu.VMEM((slots, sub_count, channels, time_length), jnp.bfloat16),
             pltpu.VMEM((slots, 1, PANEL), jnp.int32),
             pltpu.VMEM((lag_count, PANEL, time_length), jnp.bfloat16),
+            pltpu.VMEM((lag_count + 1, width), jnp.float32),
             dma((chip_count,)),
             dma((slots, chip_count)),
             dma((slots, chip_count)),
@@ -321,12 +326,10 @@
         compiler_params=pltpu.CompilerParams(collective_id=0, has_side_effects=True),
     )(
         strain,
-        fir_taps.astype(jnp.float32).reshape(1, TAPS),
+        fir_taps,
         live_mask.reshape(1, PANEL),
-        offset_band,
-    )
-    stack, count = sums[:lag_count], sums[lag_count : lag_count + 1]
-    return (stack / jnp.maximum(count, 1.0) / math.sqrt(time_length))[None]
+        jnp.swapaxes(offset_band, 1, 2),
+    )
 
 
 def solution(mesh):

time: 21.5 us -> 18.5 us (0.86)
  other arithmetic: 2.83 us -> 0 us
    broadcast_in_dim x1 -> x0, other arithmetic: 1.47 us -> none  [on_device(): return (stack / jnp.maximum(count, 1.0) / math.sqrt(time_length))[None]]
    max x1 -> x0, other arithmetic: 0.85 us -> none  [on_device(): return (stack / jnp.maximum(count, 1.0) / math.sqrt(time_length))[None]]
    reshape x1 -> x0, other arithmetic: 0.51 us -> none  [on_device(): fir_taps.astype(jnp.float32).reshape(1, TAPS)]
    unnamed x5 -> x1, local copies, waits for them, and re-layouts: 1.49 us -> 1.38 us
where the time goes in v1:
time: 18.5 us; the launch traced here: 18.2 us
  Pallas kernels  16.8 us (91%)
  local copies, waits for them, and re-layouts  1.38 us (7%)
    pallas_call x1, Pallas kernels, on_device(): pl.pallas_call(functools.partial(kernel, panel_count, sub_count, reach),...  16.8 us
    unnamed x1, local copies, waits for them, and re-layouts  1.38 us

profile of v1, /device:TPU:9, one launch (start us, length us, event | category | flops | bytes accessed | tf_op | source)
XLA Modules:
  0.0 18.2 jit_solution(8883637328819612293)
XLA Ops:
  0.0 16.8 %shard_map.46 = f32[1,4,2048]{2,1,0:T(4,128)} custom-call(bf16[128,2048]{1,0:T(8,128)(2,1)} %strain_ref.1, bf16[128]{0:T(256)(128)(2,1)} %taps_ref.1, s32[1,512]{1,0:T(1,128)} %bitcast.2, s32[1,2,3]{2,1,0:T(2,128)} %bitcast.3), custom_call_target="tpu_custom_call" | custom-call | tf_op jit(solution)/shard_map/pallas_call | solution.py:309
  16.8 1.4 %copy.6 = f32[1,4,2048]{2,1,0:T(4,128)} copy(f32[1,4,2048]{2,1,0:T(4,128)} %shard_map.46) | data formatting | bytes 65536

commit v2 on v1

--- a/solution.py
+++ b/solution.py
@@ -13,6 +13,7 @@
 TAPS = 128
 LAGS = 16
 LANES = 128
+CHUNKS = 2
 MESH = pl.DeviceIdType.MESH
 
 
@@ -76,11 +77,13 @@
     panel_count,
     sub_count,
     reach,
-    strain_ref,
+    strain_hbm,
     taps_ref,
     live_ref,
     band_ref,
     out_ref,
+    strain_ref,
+    fetched,
     panels,
     lives,
     lagged,
@@ -109,6 +112,8 @@
     def chip_at(step):
         return lax.rem(chip + step, chip_count)
 
+    fetch = pltpu.make_async_copy(strain_hbm, strain_ref, fetched)
+    fetch.start()
     barrier = pltpu.get_barrier_semaphore()
     pl.semaphore_signal(barrier, inc=1, device_id={"sub": partner}, device_id_type=MESH)
     for step in range(1, chip_count):
@@ -123,6 +128,7 @@
                 barrier, inc=1, device_id={"blk": position + d}, device_id_type=MESH
             )
 
+    fetch.wait()
     row = lax.broadcasted_iota(jnp.int32, (channels, PANEL), 0)
     column = lax.broadcasted_iota(jnp.int32, (channels, PANEL), 1)
     live_row = live_ref[...].astype(jnp.float32)
@@ -138,34 +144,45 @@
         + jnp.minimum(panel_count - 1 - position, reach),
     )
 
-    def across(step):
+    rows = channels // CHUNKS
+
+    def shard_at(step):
+        return chip_at(step) * 2 + core
+
+    def other_at(step):
+        return chip_at(step) * 2 + 1 - core
+
+    def part(slot, shard, chunk):
+        return panels.at[slot, shard, pl.ds(chunk * rows, rows)]
+
+    def across(d, step, chunk):
         return pltpu.make_async_remote_copy(
-            src_ref=panels.at[reach, me],
-            dst_ref=panels.at[reach, me],
-            send_sem=across_send.at[step],
-            recv_sem=arrival.at[reach, me],
-            device_id={"sub": chip_at(step) * 2 + core},
+            src_ref=part(d + reach, me, chunk),
+            dst_ref=part(d + reach, me, chunk),
+            send_sem=across_send.at[d + reach, step, chunk],
+            recv_sem=arrival.at[d + reach, me, chunk],
+            device_id={"sub": shard_at(step)},
             device_id_type=MESH,
         )
 
-    def to_partner(d, step):
-        shard = chip_at(step) * 2 + core
+    def to_partner(d, step, chunk):
+        shard = shard_at(step)
         return pltpu.make_async_remote_copy(
-            src_ref=panels.at[d + reach, shard],
-            dst_ref=panels.at[d + reach, shard],
-            send_sem=partner_send.at[d + reach, step],
-            recv_sem=arrival.at[d + reach, shard],
+            src_ref=part(d + reach, shard, chunk),
+            dst_ref=part(d + reach, shard, chunk),
+            send_sem=partner_send.at[d + reach, step, chunk],
+            recv_sem=arrival.at[d + reach, shard, chunk],
             device_id={"sub": partner},
             device_id_type=MESH,
         )
 
-    def along(d, step):
-        shard = chip_at(step) * 2 + core
+    def along(d, step, chunk):
+        shard = shard_at(step)
         return pltpu.make_async_remote_copy(
-            src_ref=panels.at[reach, shard],
-            dst_ref=panels.at[reach - d, shard],
-            send_sem=along_send.at[d + reach, step],
-            recv_sem=arrival.at[reach - d, shard],
+            src_ref=part(reach, shard, chunk),
+            dst_ref=part(reach - d, shard, chunk),
+            send_sem=along_send.at[d + reach, step, chunk],
+            recv_sem=arrival.at[reach - d, shard, chunk],
             device_id={"blk": position + d},
             device_id_type=MESH,
         )
@@ -180,21 +197,22 @@
             device_id_type=MESH,
         )
 
-    def arrived(d, shard):
-        pltpu.make_async_copy(
-            panels.at[d + reach, shard], panels.at[d + reach, shard], arrival.at[d + reach, shard]
-        ).wait()
-
-    for step in range(1, chip_count):
-        across(step).start()
+    def arrived(d, shard, chunk):
+        view = part(d + reach, shard, chunk)
+        pltpu.make_async_copy(view, view, arrival.at[d + reach, shard, chunk]).wait()
+
+    for chunk in range(CHUNKS):
+        for step in range(1, chip_count):
+            across(0, step, chunk).start()
     for d in distances:
 
         @pl.when(inside(d))
         def _():
-            along(d, 0).start()
+            for chunk in range(CHUNKS):
+                along(d, 0, chunk).start()
             along_live(d).start()
-
-    to_partner(0, 0).start()
+    for chunk in range(CHUNKS):
+        to_partner(0, 0, chunk).start()
 
     own_row = lax.broadcasted_iota(jnp.int32, (PANEL, PANEL), 0)
     own_column = lax.broadcasted_iota(jnp.int32, (PANEL, PANEL), 1)
@@ -203,35 +221,48 @@
     )
     sums[...] = jnp.zeros_like(sums)
 
-    for step in range(1, chip_count):
-        arrived(0, chip_at(step) * 2 + core)
-        to_partner(0, step).start()
-        for d in distances:
-
-            @pl.when(inside(d))
-            def _():
-                along(d, step).start()
-
+    first_lag = me * lag_count
+
+    def delay_chip(step):
+        visitor = chip_at(step)
+        own = panels[reach, pl.ds(visitor * 2, 2)].reshape(2 * channels, time_length)
+        own = own.astype(jnp.float32)
+        chunks = [own[:, i : i + LANES] for i in range(0, time_length, LANES)]
+        chunks = shift_right(chunks, first_lag)
+        target = pl.ds(pl.multiple_of(visitor * 2 * channels, 2 * channels), 2 * channels)
+        for lag in range(lag_count):
+            if lag:
+                chunks = shift_right(chunks, 1)
+            lagged[lag, target] = jnp.concatenate(chunks, axis=1).astype(jnp.bfloat16)
+
+    for chunk in range(CHUNKS):
+        arrived(0, other_at(0), chunk)
+    delay_chip(0)
+
+    for chunk in range(CHUNKS):
+        for step in range(1, chip_count):
+            arrived(0, shard_at(step), chunk)
+            for d in distances:
+
+                @pl.when(inside(d))
+                def _():
+                    along(d, step, chunk).start()
+
+            to_partner(0, step, chunk).start()
     for d in distances:
 
         @pl.when(inside(d))
         def _():
-            arrived(d, me)
-            to_partner(d, 0).start()
-
-    for step in range(chip_count):
-        arrived(0, chip_at(step) * 2 + 1 - core)
-
-    first_lag = me * lag_count
-    own = panels[reach].reshape(PANEL, time_length).astype(jnp.float32)
-    chunks = [own[:, i : i + LANES] for i in range(0, time_length, LANES)]
-    chunks = shift_right(chunks, first_lag)
-    for lag in range(lag_count):
-        if lag:
-            chunks = shift_right(chunks, 1)
-        lagged[lag] = jnp.concatenate(chunks, axis=1).astype(jnp.bfloat16)
-
-    def correlate(d):
+            for chunk in range(CHUNKS):
+                arrived(d, me, chunk)
+                to_partner(d, 0, chunk).start()
+
+    for step in range(1, chip_count):
+        for chunk in range(CHUNKS):
+            arrived(0, other_at(step), chunk)
+        delay_chip(step)
+
+    def totals_of(d):
         visiting = panels[d + reach].reshape(PANEL, time_length)
         rows = []
         for lag in range(lag_count):
@@ -244,7 +275,9 @@
             rows.append(diagonal_totals(correlation))
         flags = live_ref[...] if d == 0 else lives[d + reach]
         rows.append(diagonal_totals(live_column * flags.astype(jnp.float32)))
-        totals = jnp.concatenate(rows, axis=0)
+        return jnp.concatenate(rows, axis=0)
+
+    def accumulate(d, totals):
         offset = (
             lax.broadcasted_iota(jnp.int32, totals.shape, 1) + d * PANEL - (PANEL - 1)
         )
@@ -256,42 +289,63 @@
         window = (slice(0, lag_count + 1), slice(start, start + 2 * PANEL))
         sums[window] += jnp.where(kept, totals, 0.0)
 
-    correlate(0)
-
-    for step in range(1, chip_count):
+    accumulate(0, totals_of(0))
+
+    for chunk in range(CHUNKS):
         for d in distances:
 
             @pl.when(inside(d))
             def _():
-                arrived(d, chip_at(step) * 2 + core)
-                to_partner(d, step).start()
-
-    for d in distances:
-
-        @pl.when(inside(d))
+                for step in range(1, chip_count):
+                    arrived(d, shard_at(step), chunk)
+                    to_partner(d, step, chunk).start()
+
+    def settle(d):
+        for step in range(chip_count):
+            for chunk in range(CHUNKS):
+                arrived(d, other_at(step), chunk)
+        pltpu.make_async_copy(
+            lives.at[d + reach], lives.at[d + reach], live_arrival.at[d + reach]
+        ).wait()
+
+    for near in range(0, len(distances), 2):
+        pair = distances[near : near + 2]
+        both = jnp.logical_and(inside(pair[0]), inside(pair[1]))
+
+        @pl.when(both)
         def _():
-            for step in range(chip_count):
-                arrived(d, chip_at(step) * 2 + 1 - core)
-            pltpu.make_async_copy(
-                lives.at[d + reach], lives.at[d + reach], live_arrival.at[d + reach]
-            ).wait()
-            correlate(d)
+            for d in pair:
+                settle(d)
+            found = [totals_of(d) for d in pair]
+            for d, totals in zip(pair, found):
+                accumulate(d, totals)
+
+        for d in pair:
+
+            @pl.when(jnp.logical_and(inside(d), jnp.logical_not(both)))
+            def _():
+                settle(d)
+                accumulate(d, totals_of(d))
 
     inverse = 1.0 / (jnp.maximum(sums[lag_count:], 1.0) * math.sqrt(time_length))
     out_ref[0] = sums[:lag_count] * inverse
 
-    for step in range(1, chip_count):
-        across(step).wait_send()
-    for step in range(chip_count):
-        to_partner(0, step).wait_send()
+    for chunk in range(CHUNKS):
+        for step in range(1, chip_count):
+            across(0, step, chunk).wait_send()
+        for step in range(chip_count):
+            to_partner(0, step, chunk).wait_send()
     for d in distances:
 
         @pl.when(inside(d))
         def _():
             along_live(d).wait_send()
-            for step in range(chip_count):
-                along(d, step).wait_send()
-                to_partner(d, step).wait_send()
+            for chunk in range(CHUNKS):
+                along(d, 0, chunk).wait_send()
+                for step in range(1, chip_count):
+                    along(d, step, chunk).wait_send()
+                for step in range(chip_count):
+                    to_partner(d, step, chunk).wait_send()
 
 
 def on_device(strain, fir_taps, live_mask, offset_band):
@@ -309,21 +363,25 @@
     return pl.pallas_call(
         functools.partial(kernel, panel_count, sub_count, reach),
         out_shape=jax.ShapeDtypeStruct((1, lag_count, width), jnp.float32),
-        in_specs=[vmem, vmem, vmem, pl.BlockSpec(memory_space=pltpu.SMEM)],
+        in_specs=[pl.BlockSpec(memory_space=pl.ANY), vmem, vmem, pl.BlockSpec(memory_space=pltpu.SMEM)],
         out_specs=vmem,
         scratch_shapes=[
+            pltpu.VMEM((channels, raw_length), jnp.bfloat16),
+            dma,
             pltpu.VMEM((slots, sub_count, channels, time_length), jnp.bfloat16),
             pltpu.VMEM((slots, 1, PANEL), jnp.int32),
             pltpu.VMEM((lag_count, PANEL, time_length), jnp.bfloat16),
             pltpu.VMEM((lag_count + 1, width), jnp.float32),
-            dma((chip_count,)),
-            dma((slots, chip_count)),
-            dma((slots, chip_count)),
+            dma((slots, chip_count, CHUNKS)),
+            dma((slots, chip_count, CHUNKS)),
+            dma((slots, chip_count, CHUNKS)),
             dma((slots,)),
-            dma((slots, sub_count)),
+            dma((slots, sub_count, CHUNKS)),
             dma((slots,)),
         ],
-        compiler_params=pltpu.CompilerParams(collective_id=0, has_side_effects=True),
+        compiler_params=pltpu.CompilerParams(
+            collective_id=0, has_side_effects=True, vmem_limit_bytes=24 << 20
+        ),
     )(
         strain,
         fir_taps,

time: 18.5 us -> 18.3 us (0.989)
  Pallas kernels: 16.8 us -> 15.7 us
  local copies, waits for them, and re-layouts: 1.38 us -> 2.35 us
    pallas_call x1, Pallas kernels: 16.8 us -> 15.7 us  [on_device(): pl.pallas_call(functools.partial(kernel, panel_count, sub_count, reach),...]
    unnamed x1 -> x9, local copies, waits for them, and re-layouts: 1.38 us -> 2.35 us
where the time goes in v2:
time: 18.3 us; the launch traced here: 18.1 us
  Pallas kernels  15.7 us (86%)
  local copies, waits for them, and re-layouts  2.35 us (13%)
    pallas_call x1, Pallas kernels, on_device(): pl.pallas_call(functools.partial(kernel, panel_count, sub_count, reach),...  15.7 us
    unnamed x9, local copies, waits for them, and re-layouts  2.35 us

profile of v2, /device:TPU:9, one launch (start us, length us, event | category | flops | bytes accessed | tf_op | source)
XLA Modules:
  0.0 18.1 jit_solution(6731339387271423922)
XLA Ops:
  0.0 0.0 copy-start.1
  0.0 0.0 copy-start.2
  0.0 0.0 copy-start.3
  0.0 0.7 %copy-done.1 = s32[512]{0:T(512)S(1)} copy-done((s32[512]{0:T(512)S(1)}, s32[512]{0:T(512)}, u32[]{:S(2)}) %copy-start.1) | copy-done | bytes 2072
  0.7 0.0 copy-done.2
  0.7 0.0 copy-done.3
  0.7 0.0 copy-start
  0.7 1.0 %copy-done = bf16[128,2048]{1,0:T(8,128)(2,1)S(1)} copy-done((bf16[128,2048]{1,0:T(8,128)(2,1)S(1)}, bf16[128,2048]{1,0:T(8,128)(2,1)}, u32[]{:S(2)}) %copy-start) | copy-done | bytes 524312
  1.7 15.7 %shard_map.46 = f32[1,4,2048]{2,1,0:T(4,128)S(1)} custom-call(bf16[128,2048]{1,0:T(8,128)(2,1)S(1)} %copy-done, bf16[128]{0:T(256)(128)(2,1)S(1)} %copy-done.3, s32[1,512]{1,0:T(1,128)S(1)} %bitcast.2, s32[1,2,3]{2,1,0:T(2,128)S(1)} %bitcast.3), custom_call_target="tpu_custom_call" | custom-call | tf_op jit(solution)/shard_map/pallas_call | solution.py:363
  17.5 0.6 %copy.6 = f32[1,4,2048]{2,1,0:T(4,128)} copy(f32[1,4,2048]{2,1,0:T(4,128)S(1)} %shard_map.46) | data formatting | bytes 65536
Async XLA Ops:
  0.0 0.7 %copy-start.1 = (s32[512]{0:T(512)S(1)}, s32[512]{0:T(512)}, u32[]{:S(2)}) copy-start(s32[512]{0:T(512)} %param.6) | copy-start | bytes 6148
  0.0 0.7 %copy-start.2 = (s32[1,3,2]{1,2,0:T(2,128)S(1)}, s32[1,3,2]{1,2,0:T(2,128)}, u32[]{:S(2)}) copy-start(s32[1,3,2]{1,2,0:T(2,128)} %param.7) | copy-start | bytes 76
  0.0 0.7 %copy-start.3 = (bf16[128]{0:T(256)(128)(2,1)S(1)}, bf16[128]{0:T(256)(128)(2,1)}, u32[]{:S(2)}) copy-start(bf16[128]{0:T(256)(128)(2,1)} %taps_ref.1) | copy-start | bytes 772
  0.7 1.0 %copy-start = (bf16[128,2048]{1,0:T(8,128)(2,1)S(1)}, bf16[128,2048]{1,0:T(8,128)(2,1)}, u32[]{:S(2)}) copy-start(bf16[128,2048]{1,0:T(8,128)(2,1)} %strain_hbm.1) | copy-start | bytes 1572868
